TPU v7x, 32 devices: a whole 2x2x4 slice. The times are simulated.
32 devices in a mesh: dp: 4 (over y, x), seq: 8 (over z, core).
Axes of the slice: x: 2, y: 2, z: 4, core: 2. Of those that a mesh axis runs over, the one named last changes fastest.
Arguments:
- hidden_in: bfloat16 [8, 1024, 1536], P('dp', 'seq'), may hold values from -6 to 6
- lengths: int32 [8], P('dp'), may hold values from 256 to 1024, as said below
- cotangent: bfloat16 [8, 1024, 1536], P('dp', 'seq'), may hold values from -6 to 6
- attn_gain: bfloat16 [1536], P(('dp', 'seq')), may hold values from 0.25 to 1.75
- q_weight: bfloat16 [1536, 1536], P(('dp', 'seq')), may hold values from -0.15625 to 0.15625
- q_bias: bfloat16 [1536], P(('dp', 'seq')), may hold values from -3 to 3
- k_weight: bfloat16 [256, 1536], P(('dp', 'seq')), may hold values from -0.15625 to 0.15625
- k_bias: bfloat16 [256], P(('dp', 'seq')), may hold values from -3 to 3
- v_weight: bfloat16 [256, 1536], P(('dp', 'seq')), may hold values from -0.15625 to 0.15625
- v_bias: bfloat16 [256], P(('dp', 'seq')), may hold values from -0.59765625 to 0.59765625
- o_weight: bfloat16 [1536, 1536], P(('dp', 'seq')), may hold values from -0.875 to 0.875
- mlp_gain: bfloat16 [1536], P(('dp', 'seq')), may hold values from 0.25 to 1.75
- gate_weight: bfloat16 [8960, 1536], P(('dp', 'seq')), may hold values from -0.15625 to 0.15625
- up_weight: bfloat16 [8960, 1536], P(('dp', 'seq')), may hold values from -0.15625 to 0.15625
- down_weight: bfloat16 [1536, 8960], P(None, ('dp', 'seq')), may hold values from -0.0625 to 0.0625
Outputs:
- block_out: bfloat16 [8, 1024, 1536], P('dp', 'seq')
- input_grad: float32 [8, 1024, 1536], P('dp', 'seq')
- attn_gain_grad: float32 [1536], P(('dp', 'seq'))
- q_weight_grad: float32 [1536, 1536], P(('dp', 'seq'))
- q_bias_grad: float32 [1536], P(('dp', 'seq'))
- k_weight_grad: float32 [256, 1536], P(('dp', 'seq'))
- k_bias_grad: float32 [256], P(('dp', 'seq'))
- v_weight_grad: float32 [256, 1536], P(('dp', 'seq'))
- v_bias_grad: float32 [256], P(('dp', 'seq'))
- o_weight_grad: float32 [1536, 1536], P(('dp', 'seq'))
- mlp_gain_grad: float32 [1536], P(('dp', 'seq'))
- gate_weight_grad: float32 [8960, 1536], P(('dp', 'seq'))
- up_weight_grad: float32 [8960, 1536], P(('dp', 'seq'))
- down_weight_grad: float32 [1536, 8960], P(None, ('dp', 'seq'))
Inputs may be any that keep to these rules, and one draw needn't show every extreme that they name: Slots t < lengths[b] of sequence b are valid; in every draw at least one sequence is valid in all 1024 slots.
All inputs are finite; a program needn't handle non-finite values.
Results may differ from a plain program's by a relative error of at most 0.025.
Values may be sent and summed in bfloat16 or wider, within the bound.
No kernel may reach another device: no remote copies, remote signals or barrier semaphores. Data moves between devices by JAX's collectives and lax.ppermute only.
A program may use at most 448 MiB of HBM per device.

v0:
```python
import math
import jax
import jax.numpy as jnp
from jax import lax
from jax.sharding import PartitionSpec as P

HEADS = 12
KV_HEADS = 2
HEAD = 128
EPSILON = 1e-06
NEGATIVE = -1e30


def times_transposed(left_side, right_side):
    return lax.dot_general(
        left_side, right_side, (((1,), (1,)), ((), ())), preferred_element_type=jnp.float32
    )


def plain_product(left_side, right_side):
    return jnp.dot(left_side, right_side, preferred_element_type=jnp.float32)


def split_columns(values, group_count):
    row_count, width = values.shape
    return values.reshape(row_count, group_count, width // group_count)


def owner_grad(columns, inputs_all):
    part_grad = jnp.einsum("rpf,rd->pfd", columns, inputs_all, preferred_element_type=jnp.float32)
    return part_grad.reshape(-1, inputs_all.shape[1])


def owner_bias(columns):
    return jnp.sum(columns.astype(jnp.float32), axis=0).reshape(-1)


def rope_tables(positions):
    half_size = HEAD // 2
    inverse = jnp.exp(-math.log(1000000.0) * 2.0 * jnp.arange(half_size).astype(jnp.float32) / HEAD)
    angles = positions[:, None] * inverse[None, :]
    angles = jnp.concatenate([angles, angles], axis=1)
    return (jnp.cos(angles), jnp.sin(angles))


def rotate(values, cosine, sine_table):
    half_size = HEAD // 2
    turned = jnp.concatenate([-values[..., half_size:], values[..., :half_size]], axis=-1)
    return values * cosine[:, None, :] + turned * sine_table[:, None, :]


def rotate_back(gradient, cosine, sine_table):
    half_size = HEAD // 2
    scaled = gradient * sine_table[:, None, :]
    turned = jnp.concatenate([scaled[..., half_size:], -scaled[..., :half_size]], axis=-1)
    return gradient * cosine[:, None, :] + turned


def rms_parts(values):
    inverse = lax.rsqrt(jnp.mean(values * values, axis=-1, keepdims=True) + EPSILON)
    return (values * inverse, inverse)


def rms_back(upstream, normal_values, inverse, gain_values):
    scaled = upstream * gain_values
    gain_grad = jnp.sum(upstream * normal_values, axis=0)
    input_part = inverse * (
        scaled - normal_values * jnp.mean(scaled * normal_values, axis=-1, keepdims=True)
    )
    return (input_part, gain_grad)


def masked_scores(query_heads, key_heads, causal, score_scale):
    scores = (
        jnp.einsum("qkgd,skd->kgqs", query_heads, key_heads, preferred_element_type=jnp.float32)
        * score_scale
    )
    return jnp.where(causal[None, None], scores, NEGATIVE)


def on_device(
    hidden_in,
    lengths,
    cotangent,
    attn_gain,
    q_weight,
    q_bias,
    k_weight,
    k_bias,
    v_weight,
    v_bias,
    o_weight,
    mlp_gain,
    gate_weight,
    up_weight,
    down_weight,
):
    micro_count, span_rows, model_width = hidden_in.shape
    rows = micro_count * span_rows
    full_len = span_rows * lax.axis_size("seq")
    dp_count = lax.axis_size("dp")
    group_share = HEADS // KV_HEADS
    kv_width = KV_HEADS * HEAD
    score_scale = 1.0 / math.sqrt(HEAD)
    positions = lax.axis_index("seq") * span_rows + jnp.arange(span_rows, dtype=jnp.int32)
    cosine, sine_table = rope_tables(positions.astype(jnp.float32))
    causal = positions[:, None] >= jnp.arange(full_len, dtype=jnp.int32)[None, :]
    gathered = (
        lax.all_gather(attn_gain, ("dp", "seq"), axis=0, tiled=True),
        lax.all_gather(q_weight, ("dp", "seq"), axis=0, tiled=True),
        lax.all_gather(q_bias, ("dp", "seq"), axis=0, tiled=True),
        lax.all_gather(k_weight, ("dp", "seq"), axis=0, tiled=True),
        lax.all_gather(k_bias, ("dp", "seq"), axis=0, tiled=True),
        lax.all_gather(v_weight, ("dp", "seq"), axis=0, tiled=True),
        lax.all_gather(v_bias, ("dp", "seq"), axis=0, tiled=True),
        lax.all_gather(o_weight, ("dp", "seq"), axis=0, tiled=True),
        lax.all_gather(mlp_gain, ("dp", "seq"), axis=0, tiled=True),
    )
    gain_one, query_w, query_b, key_w, key_b, value_w, value_b, output_w, gain_two = gathered
    inputs = hidden_in.reshape(rows, model_width).astype(jnp.float32)
    normal_one, inverse_one = rms_parts(inputs)
    attn_in = (normal_one * gain_one.astype(jnp.float32)).astype(jnp.bfloat16)
    query_lin = times_transposed(attn_in, query_w) + query_b.astype(jnp.float32)
    key_lin = times_transposed(attn_in, key_w) + key_b.astype(jnp.float32)
    value_lin = times_transposed(attn_in, value_w) + value_b.astype(jnp.float32)
    query_rot = rotate(
        query_lin.reshape(micro_count, span_rows, HEADS, HEAD), cosine, sine_table
    ).astype(jnp.bfloat16)
    key_rot = (
        rotate(key_lin.reshape(micro_count, span_rows, KV_HEADS, HEAD), cosine, sine_table)
        .astype(jnp.bfloat16)
        .reshape(micro_count, span_rows, kv_width)
    )
    value_low = value_lin.astype(jnp.bfloat16).reshape(micro_count, span_rows, kv_width)
    key_all, value_all = (
        lax.all_gather(key_rot, "seq", axis=1, tiled=True),
        lax.all_gather(value_low, "seq", axis=1, tiled=True),
    )
    query_heads = query_rot.reshape(micro_count, span_rows, KV_HEADS, group_share, HEAD)
    key_heads = key_all.reshape(micro_count, full_len, KV_HEADS, HEAD)
    value_heads = value_all.reshape(micro_count, full_len, KV_HEADS, HEAD)
    mixed_parts = []
    log_parts = []
    for batch_index in range(micro_count):
        scores = masked_scores(
            query_heads[batch_index], key_heads[batch_index], causal, score_scale
        )
        row_top = jnp.max(scores, axis=-1, keepdims=True)
        exponent = jnp.exp(scores - row_top)
        row_total = jnp.sum(exponent, axis=-1, keepdims=True)
        log_parts.append(row_top + jnp.log(row_total))
        soft_low = (exponent / row_total).astype(jnp.bfloat16)
        mixed_heads = jnp.einsum(
            "kgqs,skd->qkgd", soft_low, value_heads[batch_index], preferred_element_type=jnp.float32
        )
        mixed_parts.append(mixed_heads.reshape(span_rows, model_width))
    mixed_low = jnp.concatenate(mixed_parts, axis=0).astype(jnp.bfloat16)
    resid = inputs + times_transposed(mixed_low, output_w)
    normal_two, inverse_two = rms_parts(resid)
    mlp_in = (normal_two * gain_two.astype(jnp.float32)).astype(jnp.bfloat16)
    gate_w, up_w, down_w = (
        lax.all_gather(gate_weight, ("dp", "seq"), axis=0, tiled=True),
        lax.all_gather(up_weight, ("dp", "seq"), axis=0, tiled=True),
        lax.all_gather(down_weight, ("dp", "seq"), axis=1, tiled=True),
    )
    gate_lin = times_transposed(mlp_in, gate_w)
    up_lin = times_transposed(mlp_in, up_w)
    gate_sigma = jax.nn.sigmoid(gate_lin)
    hidden_low = (gate_lin * gate_sigma * up_lin).astype(jnp.bfloat16)
    result = resid + times_transposed(hidden_low, down_w)
    valid_rows = (positions[None, :] < lengths[:, None]).reshape(rows)
    block_out = (
        jnp.where(valid_rows[:, None], result, 0.0)
        .astype(jnp.bfloat16)
        .reshape(micro_count, span_rows, model_width)
    )
    back_query, back_key, back_value, back_output, back_gate, back_up, back_down = (
        lax.all_gather(q_weight, ("dp", "seq"), axis=0, tiled=True),
        lax.all_gather(k_weight, ("dp", "seq"), axis=0, tiled=True),
        lax.all_gather(v_weight, ("dp", "seq"), axis=0, tiled=True),
        lax.all_gather(o_weight, ("dp", "seq"), axis=0, tiled=True),
        lax.all_gather(gate_weight, ("dp", "seq"), axis=0, tiled=True),
        lax.all_gather(up_weight, ("dp", "seq"), axis=0, tiled=True),
        lax.all_gather(down_weight, ("dp", "seq"), axis=1, tiled=True),
    )
    upstream = jnp.where(
        valid_rows[:, None], cotangent.reshape(rows, model_width).astype(jnp.float32), 0.0
    )
    upstream_low = upstream.astype(jnp.bfloat16)
    attn_all, mixed_all, mlp_all, upstream_all = (
        lax.all_gather(attn_in, "seq", axis=0, tiled=True),
        lax.all_gather(mixed_low, "seq", axis=0, tiled=True),
        lax.all_gather(mlp_in, "seq", axis=0, tiled=True),
        lax.all_gather(upstream_low, "seq", axis=0, tiled=True),
    )
    hidden_grad = plain_product(upstream_low, back_down)
    gate_grad = (
        hidden_grad * up_lin * (gate_sigma * (1.0 + gate_lin * (1.0 - gate_sigma)))
    ).astype(jnp.bfloat16)
    up_grad = (hidden_grad * gate_lin * gate_sigma).astype(jnp.bfloat16)
    mlp_in_grad = plain_product(gate_grad, back_gate) + plain_product(up_grad, back_up)
    hidden_cols, gate_cols, up_cols = (
        lax.all_to_all(
            split_columns(hidden_low, dp_count), "seq", split_axis=2, concat_axis=0, tiled=True
        ),
        lax.all_to_all(
            split_columns(gate_grad, dp_count), "seq", split_axis=2, concat_axis=0, tiled=True
        ),
        lax.all_to_all(
            split_columns(up_grad, dp_count), "seq", split_axis=2, concat_axis=0, tiled=True
        ),
    )
    down_grad = jnp.einsum(
        "rd,rpf->dpf", upstream_all, hidden_cols, preferred_element_type=jnp.float32
    ).reshape(model_width, -1)
    gate_w_grad = owner_grad(gate_cols, mlp_all)
    up_w_grad = owner_grad(up_cols, mlp_all)
    norm_two_grad, gain_two_grad = rms_back(
        mlp_in_grad, normal_two, inverse_two, gain_two.astype(jnp.float32)
    )
    resid_grad = upstream + norm_two_grad
    resid_low = resid_grad.astype(jnp.bfloat16)
    mixed_grad = (
        plain_product(resid_low, back_output)
        .astype(jnp.bfloat16)
        .reshape(micro_count, span_rows, KV_HEADS, group_share, HEAD)
    )
    query_parts = []
    key_parts = []
    value_parts = []
    for batch_index in range(micro_count):
        again_scores = masked_scores(
            query_heads[batch_index], key_heads[batch_index], causal, score_scale
        )
        soft_probs = jnp.exp(again_scores - log_parts[batch_index])
        probs_low = soft_probs.astype(jnp.bfloat16)
        prob_grad = jnp.einsum(
            "qkgd,skd->kgqs",
            mixed_grad[batch_index],
            value_heads[batch_index],
            preferred_element_type=jnp.float32,
        )
        value_all_grad = jnp.einsum(
            "kgqs,qkgd->skd", probs_low, mixed_grad[batch_index], preferred_element_type=jnp.float32
        )
        row_delta = jnp.sum(soft_probs * prob_grad, axis=-1, keepdims=True)
        score_grad = (soft_probs * (prob_grad - row_delta)).astype(jnp.bfloat16)
        query_parts.append(
            jnp.einsum(
                "kgqs,skd->qkgd",
                score_grad,
                key_heads[batch_index],
                preferred_element_type=jnp.float32,
            )
            * score_scale
        )
        key_parts.append(
            (
                jnp.einsum(
                    "kgqs,qkgd->skd",
                    score_grad,
                    query_heads[batch_index],
                    preferred_element_type=jnp.float32,
                )
                * score_scale
            ).reshape(full_len, kv_width)
        )
        value_parts.append(value_all_grad.reshape(full_len, kv_width))
    key_grad, value_grad = (
        lax.psum_scatter(jnp.stack(key_parts), "seq", scatter_dimension=1, tiled=True),
        lax.psum_scatter(jnp.stack(value_parts), "seq", scatter_dimension=1, tiled=True),
    )
    query_grad = jnp.stack(query_parts).reshape(micro_count, span_rows, HEADS, HEAD)
    query_low = (
        rotate_back(query_grad, cosine, sine_table).reshape(rows, model_width).astype(jnp.bfloat16)
    )
    key_low = (
        rotate_back(key_grad.reshape(micro_count, span_rows, KV_HEADS, HEAD), cosine, sine_table)
        .reshape(rows, kv_width)
        .astype(jnp.bfloat16)
    )
    value_grad_low = value_grad.reshape(rows, kv_width).astype(jnp.bfloat16)
    attn_in_grad = (
        plain_product(query_low, back_query)
        + plain_product(key_low, back_key)
        + plain_product(value_grad_low, back_value)
    )
    norm_one_grad, gain_one_grad = rms_back(
        attn_in_grad, normal_one, inverse_one, gain_one.astype(jnp.float32)
    )
    input_grad = (resid_grad + norm_one_grad).reshape(micro_count, span_rows, model_width)
    resid_cols, query_cols, key_cols, value_cols = (
        lax.all_to_all(
            split_columns(resid_low, dp_count), "seq", split_axis=2, concat_axis=0, tiled=True
        ),
        lax.all_to_all(
            split_columns(query_low, dp_count), "seq", split_axis=2, concat_axis=0, tiled=True
        ),
        lax.all_to_all(
            split_columns(key_low, dp_count), "seq", split_axis=2, concat_axis=0, tiled=True
        ),
        lax.all_to_all(
            split_columns(value_grad_low, dp_count), "seq", split_axis=2, concat_axis=0, tiled=True
        ),
    )
    output_w_grad = owner_grad(resid_cols, mixed_all)
    query_w_grad = owner_grad(query_cols, attn_all)
    key_w_grad = owner_grad(key_cols, attn_all)
    value_w_grad = owner_grad(value_cols, attn_all)
    query_b_grad = owner_bias(query_cols)
    key_b_grad = owner_bias(key_cols)
    value_b_grad = owner_bias(value_cols)
    totals = (
        lax.psum_scatter(
            query_w_grad.astype(jnp.bfloat16), "dp", scatter_dimension=0, tiled=True
        ).astype(jnp.float32),
        lax.psum_scatter(
            query_b_grad.astype(jnp.bfloat16), "dp", scatter_dimension=0, tiled=True
        ).astype(jnp.float32),
        lax.psum_scatter(
            key_w_grad.astype(jnp.bfloat16), "dp", scatter_dimension=0, tiled=True
        ).astype(jnp.float32),
        lax.psum_scatter(
            key_b_grad.astype(jnp.bfloat16), "dp", scatter_dimension=0, tiled=True
        ).astype(jnp.float32),
        lax.psum_scatter(
            value_w_grad.astype(jnp.bfloat16), "dp", scatter_dimension=0, tiled=True
        ).astype(jnp.float32),
        lax.psum_scatter(
            value_b_grad.astype(jnp.bfloat16), "dp", scatter_dimension=0, tiled=True
        ).astype(jnp.float32),
        lax.psum_scatter(
            output_w_grad.astype(jnp.bfloat16), "dp", scatter_dimension=0, tiled=True
        ).astype(jnp.float32),
        lax.psum_scatter(
            gate_w_grad.astype(jnp.bfloat16), "dp", scatter_dimension=0, tiled=True
        ).astype(jnp.float32),
        lax.psum_scatter(
            up_w_grad.astype(jnp.bfloat16), "dp", scatter_dimension=0, tiled=True
        ).astype(jnp.float32),
        lax.psum_scatter(
            down_grad.astype(jnp.bfloat16), "dp", scatter_dimension=1, tiled=True
        ).astype(jnp.float32),
    )
    gain_totals = (
        lax.psum_scatter(gain_one_grad, ("dp", "seq"), scatter_dimension=0, tiled=True),
        lax.psum_scatter(gain_two_grad, ("dp", "seq"), scatter_dimension=0, tiled=True),
    )
    return (
        block_out,
        input_grad,
        gain_totals[0],
        totals[0],
        totals[1],
        totals[2],
        totals[3],
        totals[4],
        totals[5],
        totals[6],
        gain_totals[1],
        totals[7],
        totals[8],
        totals[9],
    )


def solution(mesh):
    placed = (
        P("dp", "seq", None),
        P("dp"),
        P("dp", "seq", None),
        P(("dp", "seq")),
        P(("dp", "seq"), None),
        P(("dp", "seq")),
        P(("dp", "seq"), None),
        P(("dp", "seq")),
        P(("dp", "seq"), None),
        P(("dp", "seq")),
        P(("dp", "seq"), None),
        P(("dp", "seq")),
        P(("dp", "seq"), None),
        P(("dp", "seq"), None),
        P(None, ("dp", "seq")),
    )
    return jax.shard_map(
        on_device,
        mesh=mesh,
        in_specs=placed,
        out_specs=(
            P("dp", "seq", None),
            P("dp", "seq", None),
            P(("dp", "seq")),
            P(("dp", "seq"), None),
            P(("dp", "seq")),
            P(("dp", "seq"), None),
            P(("dp", "seq")),
            P(("dp", "seq"), None),
            P(("dp", "seq")),
            P(("dp", "seq"), None),
            P(("dp", "seq")),
            P(("dp", "seq"), None),
            P(("dp", "seq"), None),
            P(None, ("dp", "seq")),
        ),
        check_vma=False,
    )
```

profile of v0, /device:TPU:0, one launch (start us, length us, event | category | flops | bytes accessed | tf_op | source)
XLA Modules:
  0.0 1691.5 jit_solution(5494307519598988704)
XLA Ops:
  11.5 42.2 %all-reduce.16 = (bf16[1536]{0:T(1024)(128)(2,1)S(1)}, bf16[256]{0:T(256)(128)(2,1)S(1)}, bf16[256]{0:T(256)(128)(2,1)S(1)}, bf16[1536]{0:T(1024)(128)(2,1)S(1)}, bf16[1536]{0:T(1024)(128)(2,1)S(1)}) all-reduce(bf16[1536]{0:T(1024)(128)(2,1)S(1)} %dynamic-update-slice, ...), channel_id=1, replica_groups=mesh['dp'=4,'seq'=8] {'dp','seq'}, use_global_device_ids=true, to_apply=%add | all-reduce | flops 5120 | bytes 20480
  55.1 43.7 %all_gather.62 = bf16[256,1536]{1,0:T(8,128)(2,1)S(1)} all-gather(bf16[8,1536]{1,0:T(8,128)(2,1)} %param.23), channel_id=1, replica_groups=mesh['dp'=4,'seq'=8] {'dp','seq'}, dimensions={0}, use_global_device_ids=true | all-gather | bytes 811008 | tf_op jit(solution)/shard_map/all_gather | solution.py:114
  101.7 41.4 %all_gather.65 = bf16[256,1536]{1,0:T(8,128)(2,1)S(1)} all-gather(bf16[8,1536]{1,0:T(8,128)(2,1)S(1)} %copy-done.51), channel_id=1, replica_groups=mesh['dp'=4,'seq'=8] {'dp','seq'}, dimensions={0}, use_global_device_ids=true | all-gather | bytes 811008 | tf_op jit(solution)/shard_map/all_gather | solution.py:112
  155.0 13.8 all-gather.14.cloned.1.call-done
  171.2 63.2 %all-gather.16.cloned.1.call-done = bf16[1536,1536]{1,0:T(8,128)(2,1)} async-done(((bf16[48,1536]{1,0:T(8,128)(2,1)}), bf16[1536,1536]{1,0:T(8,128)(2,1)}) %all-gather.16.cloned.1.call-update) | async-done | bytes 4718608 | tf_op jit(solution)/shard_map/all_gather | solution.py:110
  257.0 42.2 %all-gather.18.cloned.1.call-done = bf16[1536,1536]{1,0:T(8,128)(2,1)} async-done(((bf16[48,1536]{1,0:T(8,128)(2,1)}), bf16[1536,1536]{1,0:T(8,128)(2,1)}) %all-gather.18.cloned.1.call-update) | async-done | bytes 4718608 | tf_op jit(solution)/shard_map/all_gather | solution.py:116
  303.9 161.8 %all-gather.20.cloned.1.call-done = bf16[8960,1536]{1,0:T(8,128)(2,1)} async-done(((bf16[280,1536]{1,0:T(8,128)(2,1)}), bf16[8960,1536]{1,0:T(8,128)(2,1)}) %all-gather.20.cloned.1.call-update) | async-done | bytes 27525136 | tf_op jit(solution)/shard_map/all_gather | solution.py:162
  465.8 16.7 fusion.50
  482.5 149.7 %all-gather.22.cloned.1.call-done = bf16[8960,1536]{1,0:T(8,128)(2,1)} async-done(((bf16[280,1536]{1,0:T(8,128)(2,1)}), bf16[8960,1536]{1,0:T(8,128)(2,1)}) %all-gather.22.cloned.1.call-update) | async-done | bytes 27525136 | tf_op jit(solution)/shard_map/all_gather | solution.py:163
  632.2 16.4 fusion.51
  648.7 150.2 %all-gather.24.cloned.1.call-done = bf16[1536,8960]{0,1:T(8,128)(2,1)} async-done(((bf16[1536,280]{0,1:T(8,128)(2,1)}), bf16[1536,8960]{0,1:T(8,128)(2,1)}) %all-gather.24.cloned.1.call-update) | async-done | bytes 27525136 | tf_op jit(solution)/shard_map/all_gather | solution.py:164
  798.9 20.1 %multiply_convert_fusion = (bf16[256,8960]{1,0:T(8,128)(2,1)S(1)}, bf16[256,8960]{1,0:T(8,128)(2,1)}, bf16[256,8960]{1,0:T(8,128)(2,1)}) fusion(f32[256,8960]{1,0:T(8,128)} %fusion.50, f32[256,8960]{1,0:T(8,128)} %fusion.51, bf16[256,1536]{1,0:T(8,128)(2,1)S(1)} %copy-done.24, bf16[1536,8960]{0,1:T(8,128)(2,1)} %all-gather.24.cloned.1.call-done), kind=kOutput, calls=%fused_computation | convolution fusion | flops 7083130880 | bytes 60424192 | tf_op jit(solution)/shard_map/dot_general | solution.py:21
  819.0 16.4 fusion.52
  835.5 14.8 multiply_reduce_fusion
  910.6 14.6 all-to-all-done.3
  931.8 28.9 %all-to-all-done = bf16[256,4,384]{0,1,2:T(4,128)(2,1)S(1)} async-done(((bf16[256,4,384]{0,1,2:T(4,128)(2,1)}), bf16[256,4,384]{0,1,2:T(4,128)(2,1)S(1)}, u32[]{:S(2)}, u32[]{:S(2)}) %all-to-all-start) | async-done | bytes 786464 | tf_op jit(solution)/shard_map/all_to_all | solution.py:296
  975.1 6.7 copy.145
  981.9 18.3 %copy.146 = bf16[256,4,2240]{0,1,2:T(4,128)(2,1)} copy(bf16[256,4,2240]{0,2,1:T(8,128)(2,1)} %bitcast.310) | data formatting | bytes 9175040 | tf_op jit(solution)/shard_map/reshape | solution.py:26
  1006.6 57.7 %all-gather.28.cloned.1.call-done = bf16[2048,1536]{0,1:T(8,128)(2,1)} async-done(((bf16[256,1536]{0,1:T(8,128)(2,1)}), bf16[2048,1536]{0,1:T(8,128)(2,1)}) %all-gather.28.cloned.1.call-update) | async-done | bytes 6291472 | tf_op jit(solution)/shard_map/all_gather | solution.py:192
  1076.7 18.2 %copy.150 = bf16[256,4,2240]{0,1,2:T(4,128)(2,1)} copy(bf16[256,4,2240]{0,2,1:T(8,128)(2,1)} %bitcast.311) | data formatting | bytes 9175040 | tf_op jit(solution)/shard_map/reshape | solution.py:26
  1094.9 83.9 %all-to-all-done.4 = bf16[256,4,2240]{0,1,2:T(4,128)(2,1)} async-done(((bf16[256,4,2240]{0,1,2:T(4,128)(2,1)}), bf16[256,4,2240]{0,1,2:T(4,128)(2,1)}, u32[]{:S(2)}, u32[]{:S(2)}) %all-to-all-start.4) | async-done | bytes 4587552 | tf_op jit(solution)/shard_map/all_to_all | solution.py:206
  1202.7 115.3 %all-gather.30.cloned.1.call-done = bf16[2048,1536]{1,0:T(8,128)(2,1)} async-done(((bf16[256,1536]{1,0:T(8,128)(2,1)}), bf16[2048,1536]{1,0:T(8,128)(2,1)}) %all-gather.30.cloned.1.call-update) | async-done | bytes 6291472 | tf_op jit(solution)/shard_map/all_gather | solution.py:193
  1318.0 12.0 convolution_convert_fusion.2
  1336.6 18.2 %copy.154 = bf16[256,4,2240]{0,1,2:T(4,128)(2,1)} copy(bf16[256,4,2240]{0,2,1:T(8,128)(2,1)} %bitcast.315) | data formatting | bytes 9175040 | tf_op jit(solution)/shard_map/reshape | solution.py:26
  1369.2 8.7 convolution_convert_fusion.1
  1378.2 108.3 %all-to-all-done.6 = bf16[256,4,2240]{0,1,2:T(4,128)(2,1)} async-done(((bf16[256,4,2240]{0,1,2:T(4,128)(2,1)}), bf16[256,4,2240]{0,1,2:T(4,128)(2,1)}, u32[]{:S(2)}, u32[]{:S(2)}) %all-to-all-start.6) | async-done | bytes 4587552 | tf_op jit(solution)/shard_map/all_to_all | solution.py:203
  1492.1 12.0 convolution_convert_fusion
  1512.0 14.4 fusion.19
  1536.7 37.7 %all-reduce.15 = (f32[1536]{0:T(1024)S(1)}, f32[1536]{0:T(1024)S(1)}) all-reduce(f32[1536]{0:T(1024)S(1)} %get-tuple-element.16, f32[1536]{0:T(1024)} %get-tuple-element.14), channel_id=4, replica_groups=mesh['dp'=4,'seq'=8] {'dp','seq'}, use_global_device_ids=true, to_apply=%region_13.14.clone | all-reduce | flops 3072 | bytes 24576
  1579.7 10.5 all-reduce.17
  1595.4 37.4 %reduce-scatter.24.cloned.1.call-done = bf16[280,1536]{1,0:T(8,128)(2,1)} async-done(((bf16[1120,1536]{1,0:T(8,128)(2,1)}), bf16[280,1536]{1,0:T(8,128)(2,1)}) %reduce-scatter.24.cloned.1.call-update) | async-done | bytes 860176
  1635.3 46.9 %reduce-scatter.26.cloned.1.call-done = bf16[1536,280]{0,1:T(8,128)(2,1)} async-done(((bf16[1536,1120]{0,1:T(8,128)(2,1)}), bf16[1536,280]{0,1:T(8,128)(2,1)}) %reduce-scatter.26.cloned.1.call-update) | async-done | bytes 860176
  (351 shorter events, 232.1 us)
Async XLA Ops:
  7.2 144.6 %all-gather.12.cloned.1.call-start = ((), (), s32[]{:S(2)}) async-start(), calls=%async_computation.14 | async-start | bytes 1179648 | tf_op jit(solution)/shard_map/all_gather | solution.py:137
  100.5 133.8 %copy-start.9 = (bf16[256,1536]{1,0:T(8,128)(2,1)}, bf16[256,1536]{1,0:T(8,128)(2,1)S(1)}, u32[]{:S(2)}) copy-start(bf16[256,1536]{1,0:T(8,128)(2,1)S(1)} %multiply_convert_fusion.4) | copy-start | bytes 2359300
  101.6 67.3 %all-gather.14.cloned.1.call-start = ((), (), s32[]{:S(2)}) async-start(), calls=%async_computation.15 | async-start | bytes 1179648 | tf_op jit(solution)/shard_map/all_gather | solution.py:136
  146.6 87.8 %all-gather.16.cloned.1.call-start = ((), (), s32[]{:S(2)}) async-start(), calls=%async_computation.16 | async-start | bytes 4866048 | tf_op jit(solution)/shard_map/all_gather | solution.py:110
  147.3 151.8 %all-gather.18.cloned.1.call-start = ((), (), s32[]{:S(2)}) async-start(), calls=%async_computation.17 | async-start | bytes 4866048 | tf_op jit(solution)/shard_map/all_gather | solution.py:116
  147.9 317.9 %all-gather.20.cloned.1.call-start = ((), (), s32[]{:S(2)}) async-start(), calls=%async_computation.18 | async-start | bytes 28385280 | tf_op jit(solution)/shard_map/all_gather | solution.py:162
  148.5 483.8 %all-gather.22.cloned.1.call-start = ((), (), s32[]{:S(2)}) async-start(), calls=%async_computation.19 | async-start | bytes 28385280 | tf_op jit(solution)/shard_map/all_gather | solution.py:163
  149.0 649.8 %all-gather.24.cloned.1.call-start = ((), (), s32[]{:S(2)}) async-start(), calls=%async_computation.20 | async-start | bytes 28385280 | tf_op jit(solution)/shard_map/all_gather | solution.py:164
  149.8 779.3 %reduce-scatter.14.cloned.1.call-start = ((), (), s32[]{:S(2)}) async-start(), calls=%async_computation.21 | async-start | bytes 2359296 | tf_op jit(solution)/shard_map/reduce_scatter | solution.py:270
  303.1 547.2 %copy-start.13 = (f32[256,1536]{1,0:T(8,128)}, f32[256,1536]{1,0:T(8,128)S(1)}, u32[]{:S(2)}) copy-start(f32[256,1536]{1,0:T(8,128)S(1)} %get-tuple-element.58) | copy-start | bytes 4718596
  303.9 328.3 %copy-start.25 = (bf16[256,1536]{1,0:T(8,128)(2,1)}, bf16[256,1536]{1,0:T(8,128)(2,1)S(1)}, u32[]{:S(2)}) copy-start(bf16[256,1536]{1,0:T(8,128)(2,1)S(1)} %multiply_convert_fusion.3) | copy-start | bytes 2359300
  482.5 316.4 %copy-start.24 = (bf16[256,1536]{1,0:T(8,128)(2,1)S(1)}, bf16[256,1536]{1,0:T(8,128)(2,1)}, u32[]{:S(2)}) copy-start(bf16[256,1536]{1,0:T(8,128)(2,1)} %fusion.24) | copy-start | bytes 2359300
  878.0 86.8 %reduce-scatter.16.cloned.1.call-start = ((), (), s32[]{:S(2)}) async-start(), calls=%async_computation.22 | async-start | bytes 2359296 | tf_op jit(solution)/shard_map/reduce_scatter | solution.py:271
  888.3 176.0 %all-gather.28.cloned.1.call-start = ((), (), s32[]{:S(2)}) async-start(), calls=%async_computation.25 | async-start | bytes 7077888 | tf_op jit(solution)/shard_map/all_gather | solution.py:192
  890.5 293.8 %all-gather.26.cloned.1.call-start = ((), (), s32[]{:S(2)}) async-start(), calls=%async_computation.23 | async-start | bytes 7077888 | tf_op jit(solution)/shard_map/all_gather | solution.py:191
  891.3 426.8 %all-gather.30.cloned.1.call-start = ((), (), s32[]{:S(2)}) async-start(), calls=%async_computation.27 | async-start | bytes 7077888 | tf_op jit(solution)/shard_map/all_gather | solution.py:193
  891.9 600.3 %all-gather.32.cloned.1.call-start = ((), (), s32[]{:S(2)}) async-start(), calls=%async_computation.28 | async-start | bytes 7077888 | tf_op jit(solution)/shard_map/all_gather | solution.py:194
  897.7 27.5 %all-to-all-start.3 = ((bf16[256,4,384]{0,1,2:T(4,128)(2,1)}), bf16[256,4,384]{0,1,2:T(4,128)(2,1)}, u32[]{:S(2)}, u32[]{:S(2)}) async-start(bf16[256,4,384]{0,1,2:T(4,128)(2,1)} %copy.142), calls=%async_computation.6 | async-start | bytes 1572864 | tf_op jit(solution)/shard_map/all_to_all | solution.py:293
  925.2 35.5 %all-to-all-start = ((bf16[256,4,384]{0,1,2:T(4,128)(2,1)}), bf16[256,4,384]{0,1,2:T(4,128)(2,1)S(1)}, u32[]{:S(2)}, u32[]{:S(2)}) async-start(bf16[256,4,384]{0,1,2:T(4,128)(2,1)} %copy.133), calls=%async_computation.2 | async-start | bytes 1572864 | tf_op jit(solution)/shard_map/all_to_all | solution.py:296
  960.7 10.9 all-to-all-start.1
  971.5 218.4 %copy-start.34 = (bf16[256,4,64]{0,1,2:T(4,128)(2,1)}, bf16[256,4,64]{0,1,2:T(4,128)(2,1)S(1)}, u32[]{:S(2)}) copy-start(bf16[256,4,64]{0,1,2:T(4,128)(2,1)S(1)} %all-to-all-done.1) | copy-start | bytes 393220
  971.5 28.6 %all-to-all-start.2 = ((bf16[256,4,64]{0,1,2:T(4,128)(2,1)}), bf16[256,4,64]{0,1,2:T(4,128)(2,1)S(1)}, u32[]{:S(2)}, u32[]{:S(2)}) async-start(bf16[256,4,64]{0,1,2:T(4,128)(2,1)} %copy.140), calls=%async_computation.5 | async-start | bytes 262144 | tf_op jit(solution)/shard_map/all_to_all | solution.py:302
  1000.2 189.8 %copy-start.36 = (bf16[256,4,64]{0,1,2:T(4,128)(2,1)}, bf16[256,4,64]{0,1,2:T(4,128)(2,1)S(1)}, u32[]{:S(2)}) copy-start(bf16[256,4,64]{0,1,2:T(4,128)(2,1)S(1)} %all-to-all-done.2) | copy-start | bytes 393220
  1000.2 178.6 %all-to-all-start.4 = ((bf16[256,4,2240]{0,1,2:T(4,128)(2,1)}), bf16[256,4,2240]{0,1,2:T(4,128)(2,1)}, u32[]{:S(2)}, u32[]{:S(2)}) async-start(bf16[256,4,2240]{0,1,2:T(4,128)(2,1)} %copy.146), calls=%async_computation.8 | async-start | bytes 9175040 | tf_op jit(solution)/shard_map/all_to_all | solution.py:206
  1005.2 522.0 %reduce-scatter.20.cloned.1.call-start = ((), (), s32[]{:S(2)}) async-start(), calls=%async_computation.26 | async-start | bytes 737280 | tf_op jit(solution)/shard_map/reduce_scatter | solution.py:332
  1178.8 180.8 %all-to-all-start.5 = ((bf16[256,4,2240]{0,1,2:T(4,128)(2,1)}), bf16[256,4,2240]{0,1,2:T(4,128)(2,1)}, u32[]{:S(2)}, u32[]{:S(2)}) async-start(bf16[256,4,2240]{0,1,2:T(4,128)(2,1)} %copy.150), calls=%async_computation.9 | async-start | bytes 9175040 | tf_op jit(solution)/shard_map/all_to_all | solution.py:209
  1184.1 344.8 %reduce-scatter.18.cloned.1.call-start = ((), (), s32[]{:S(2)}) async-start(), calls=%async_computation.24 | async-start | bytes 737280 | tf_op jit(solution)/shard_map/reduce_scatter | solution.py:314
  1189.4 402.0 %all-reduce.21.cloned.1.call-start = ((), (), s32[]{:S(2)}) async-start(), calls=%async_computation.32 | async-start | bytes 393216
  1197.1 395.7 %reduce-scatter.22.cloned.1.call-start = ((), (), s32[]{:S(2)}) async-start(), calls=%async_computation.29 | async-start | bytes 4300800
  1359.6 126.8 %all-to-all-start.6 = ((bf16[256,4,2240]{0,1,2:T(4,128)(2,1)}), bf16[256,4,2240]{0,1,2:T(4,128)(2,1)}, u32[]{:S(2)}, u32[]{:S(2)}) async-start(bf16[256,4,2240]{0,1,2:T(4,128)(2,1)} %copy.154), calls=%async_computation.10 | async-start | bytes 9175040 | tf_op jit(solution)/shard_map/all_to_all | solution.py:203
  1364.3 268.5 %reduce-scatter.24.cloned.1.call-start = ((), (), s32[]{:S(2)}) async-start(), calls=%async_computation.30 | async-start | bytes 4300800
  1378.0 304.2 %reduce-scatter.26.cloned.1.call-start = ((), (), s32[]{:S(2)}) async-start(), calls=%async_computation.31 | async-start | bytes 4300800
  (65 other events, 1005.9 us)
Sparse Core Ops, SparseCore 0:
  101.7 21.0 all-gather.11
  146.7 22.1 all-gather.13
  171.9 62.3 all-gather.15
  237.2 61.8 all-gather.17
  302.0 163.6 all-gather.19
  468.6 163.5 all-gather.21
  635.3 163.5 all-gather.23
  878.1 36.5 reduce-scatter.13
  917.1 45.6 reduce-scatter.15
  964.2 100.0 all-gather.27
  1065.9 117.1 all-gather.25
  1184.7 133.3 all-gather.29
  1320.2 101.5 all-gather.31
  1424.5 35.5 reduce-scatter.19
  1462.8 25.4 reduce-scatter.17
  1491.1 42.6 all-reduce.20
  1536.6 46.9 reduce-scatter.21
  1586.5 46.1 reduce-scatter.23
  1635.8 46.3 reduce-scatter.25
where the time goes:
time: 1700 us; the launch traced here: 1690 us
  waiting for transfers between devices  1090 us (64%)
  matrix products  199 us (12%)
  blocking collectives  176 us (10%)
  local copies, waits for them, and re-layouts  137 us (8%)
  other arithmetic  43.6 us (3%)
  starting transfers between devices  31.8 us (2%)
    all_gather x1, waiting for transfers between devices, on_device(): lax.all_gather(gate_weight, ('dp', 'seq'), axis=0, tiled=True)  162 us
    all_gather x1, waiting for transfers between devices, on_device(): lax.all_gather(down_weight, ('dp', 'seq'), axis=1, tiled=True)  150 us
    all_gather x1, waiting for transfers between devices, on_device(): lax.all_gather(up_weight, ('dp', 'seq'), axis=0, tiled=True)  150 us
    all_gather x1, waiting for transfers between devices, on_device(): lax.all_gather(mlp_in, 'seq', axis=0, tiled=True)  115 us
    all_to_all x1, waiting for transfers between devices, on_device(): lax.all_to_all(split_columns(hidden_low, dp_count), 'seq', split_axis=2,...  108 us
    unnamed x3, blocking collectives  90.4 us
    unnamed x23, waiting for transfers between devices  89.3 us
    all_to_all x1, waiting for transfers between devices, on_device(): lax.all_to_all(split_columns(gate_grad, dp_count), 'seq', split_axis=2, c...  83.9 us
  transfers between devices with their start and end apart: 26, of which 16 were waited for; matrix products, arithmetic and copies ran while one was open for 17% of the time, Pallas kernels for 0%

commit v1 on v0

--- a/solution.py
+++ b/solution.py
@@ -9,6 +9,28 @@
 HEAD = 128
 EPSILON = 1e-06
 NEGATIVE = -1e30
+
+
+def joined_along(blocks, dim):
+    shape = list(blocks.shape[1:])
+    shape[dim] *= blocks.shape[0]
+    return jnp.moveaxis(blocks, 0, dim).reshape(shape)
+
+
+def ring_gather(x, axis, dim):
+    count = lax.axis_size(axis)
+    pairs = [(i, (i + 1) % count) for i in range(count)]
+    back = [(b, a) for a, b in pairs]
+    lower, upper = ([], [])
+    for step in range(count - 1):
+        if step % 2 == 0:
+            lower.append(lax.ppermute(lower[-1] if lower else x, axis, pairs))
+        else:
+            upper.append(lax.ppermute(upper[-1] if upper else x, axis, back))
+    tiles = jnp.stack([*lower[::-1], x, *upper])
+    shift = lax.axis_index(axis) - len(lower)
+    tiles = tiles[(jnp.arange(count) - shift) % count]
+    return joined_along(tiles, dim)
 
 
 def times_transposed(left_side, right_side):
@@ -189,7 +211,7 @@
     upstream_low = upstream.astype(jnp.bfloat16)
     attn_all, mixed_all, mlp_all, upstream_all = (
         lax.all_gather(attn_in, "seq", axis=0, tiled=True),
-        lax.all_gather(mixed_low, "seq", axis=0, tiled=True),
+        ring_gather(mixed_low, "seq", 0),
         lax.all_gather(mlp_in, "seq", axis=0, tiled=True),
         lax.all_gather(upstream_low, "seq", axis=0, tiled=True),
     )

time: 1700 us -> 1680 us (0.988)
  waiting for transfers between devices: 1090 us -> 937 us
  starting transfers between devices: 31.8 us -> 134 us
  local copies, waits for them, and re-layouts: 137 us -> 159 us
    ppermute x0 -> x7, waiting for transfers between devices: none -> 177 us  [the longest x4 176 us: ring_gather(): lower.append(lax.ppermute(lower[-1] if lower else x, axis, pairs))]
    all_gather x1, waiting for transfers between devices: 115 us -> 0.01 us  [on_device(): lax.all_gather(mlp_in, 'seq', axis=0, tiled=True)]
    unnamed x23 -> x22, waiting for transfers between devices: 89.3 us -> 4.69 us
    all_to_all x1, waiting for transfers between devices: 83.9 us -> 0.01 us  [on_device(): lax.all_to_all(split_columns(gate_grad, dp_count), 'seq', split_axis=2, c...]
    all_to_all x1, starting transfers between devices: 5.27 us -> 73.4 us  [on_device(): lax.all_to_all(split_columns(up_grad, dp_count), 'seq', split_axis=2, con...]
    all_gather x1 -> x0, waiting for transfers between devices: 57.7 us -> none  [on_device(): lax.all_gather(mixed_low, 'seq', axis=0, tiled=True)]
    ppermute x0 -> x7, starting transfers between devices: none -> 34.8 us  [the longest x4 27.7 us: ring_gather(): lower.append(lax.ppermute(lower[-1] if lower else x, axis, pairs))]
    all_to_all x1, waiting for transfers between devices: 4.84 us -> 33.4 us  [on_device(): lax.all_to_all(split_columns(up_grad, dp_count), 'seq', split_axis=2, con...]
  transfers between devices with their start and end apart: 26 -> 32, of which waited for: 16 -> 16; matrix products, arithmetic and copies ran while one was open for 17% -> 19% of each run, Pallas kernels for 0% -> 0%
where the time goes in v1:
time: 1680 us; the launch traced here: 1670 us
  waiting for transfers between devices  937 us (56%)
  matrix products  200 us (12%)
  blocking collectives  176 us (10%)
  local copies, waits for them, and re-layouts  159 us (9%)
  starting transfers between devices  134 us (8%)
  other arithmetic  45.8 us (3%)
  between operations  17.1 us (1%)
    ppermute x4, waiting for transfers between devices, ring_gather(): lower.append(lax.ppermute(lower[-1] if lower else x, axis, pairs))  176 us
    all_gather x1, waiting for transfers between devices, on_device(): lax.all_gather(gate_weight, ('dp', 'seq'), axis=0, tiled=True)  162 us
    all_gather x1, waiting for transfers between devices, on_device(): lax.all_gather(up_weight, ('dp', 'seq'), axis=0, tiled=True)  150 us
    all_gather x1, waiting for transfers between devices, on_device(): lax.all_gather(down_weight, ('dp', 'seq'), axis=1, tiled=True)  149 us
    unnamed x3, blocking collectives  90.3 us
    all_to_all x1, waiting for transfers between devices, on_device(): lax.all_to_all(split_columns(hidden_low, dp_count), 'seq', split_axis=2,...  88.4 us
    all_to_all x1, starting transfers between devices, on_device(): lax.all_to_all(split_columns(up_grad, dp_count), 'seq', split_axis=2, con...  73.4 us
    all_gather x1, waiting for transfers between devices, on_device(): lax.all_gather(q_weight, ('dp', 'seq'), axis=0, tiled=True)  63.2 us
  transfers between devices with their start and end apart: 32, of which 16 were waited for; matrix products, arithmetic and copies ran while one was open for 19% of the time, Pallas kernels for 0%

profile of v1, /device:TPU:0, one launch (start us, length us, event | category | flops | bytes accessed | tf_op | source)
XLA Modules:
  0.0 1669.7 jit_solution(11730609247259682478)
XLA Ops:
  11.5 42.2 %all-reduce.16 = (bf16[1536]{0:T(1024)(128)(2,1)S(1)}, bf16[256]{0:T(256)(128)(2,1)S(1)}, bf16[256]{0:T(256)(128)(2,1)S(1)}, bf16[1536]{0:T(1024)(128)(2,1)S(1)}, bf16[1536]{0:T(1024)(128)(2,1)S(1)}) all-reduce(bf16[1536]{0:T(1024)(128)(2,1)S(1)} %dynamic-update-slice, ...), channel_id=1, replica_groups=mesh['dp'=4,'seq'=8] {'dp','seq'}, use_global_device_ids=true, to_apply=%add | all-reduce | flops 5120 | bytes 20480
  55.1 43.7 %all_gather.59 = bf16[256,1536]{1,0:T(8,128)(2,1)S(1)} all-gather(bf16[8,1536]{1,0:T(8,128)(2,1)} %param.23), channel_id=1, replica_groups=mesh['dp'=4,'seq'=8] {'dp','seq'}, dimensions={0}, use_global_device_ids=true | all-gather | bytes 811008 | tf_op jit(solution)/shard_map/all_gather | solution.py:136
  101.7 41.6 %all_gather.62 = bf16[256,1536]{1,0:T(8,128)(2,1)S(1)} all-gather(bf16[8,1536]{1,0:T(8,128)(2,1)S(1)} %copy-done.53), channel_id=1, replica_groups=mesh['dp'=4,'seq'=8] {'dp','seq'}, dimensions={0}, use_global_device_ids=true | all-gather | bytes 811008 | tf_op jit(solution)/shard_map/all_gather | solution.py:134
  154.8 14.3 all-gather.13.cloned.1.call-done
  171.3 63.2 %all-gather.15.cloned.1.call-done = bf16[1536,1536]{1,0:T(8,128)(2,1)} async-done(((bf16[48,1536]{1,0:T(8,128)(2,1)}), bf16[1536,1536]{1,0:T(8,128)(2,1)}) %all-gather.15.cloned.1.call-update) | async-done | bytes 4718608 | tf_op jit(solution)/shard_map/all_gather | solution.py:132
  257.2 42.1 %all-gather.17.cloned.1.call-done = bf16[1536,1536]{1,0:T(8,128)(2,1)} async-done(((bf16[48,1536]{1,0:T(8,128)(2,1)}), bf16[1536,1536]{1,0:T(8,128)(2,1)}) %all-gather.17.cloned.1.call-update) | async-done | bytes 4718608 | tf_op jit(solution)/shard_map/all_gather | solution.py:138
  303.5 162.4 %all-gather.19.cloned.1.call-done = bf16[8960,1536]{1,0:T(8,128)(2,1)} async-done(((bf16[280,1536]{1,0:T(8,128)(2,1)}), bf16[8960,1536]{1,0:T(8,128)(2,1)}) %all-gather.19.cloned.1.call-update) | async-done | bytes 27525136 | tf_op jit(solution)/shard_map/all_gather | solution.py:184
  465.9 16.4 fusion.52
  482.3 150.2 %all-gather.21.cloned.1.call-done = bf16[8960,1536]{1,0:T(8,128)(2,1)} async-done(((bf16[280,1536]{1,0:T(8,128)(2,1)}), bf16[8960,1536]{1,0:T(8,128)(2,1)}) %all-gather.21.cloned.1.call-update) | async-done | bytes 27525136 | tf_op jit(solution)/shard_map/all_gather | solution.py:185
  632.4 17.2 %fusion.53 = f32[256,8960]{1,0:T(8,128)} fusion(bf16[256,1536]{1,0:T(8,128)(2,1)} %copy-done.26, bf16[8960,1536]{1,0:T(8,128)(2,1)} %all-gather.21.cloned.1.call-done), kind=kOutput, calls=%fused_computation.149 | convolution fusion | flops 7046430720 | bytes 37486592 | tf_op jit(solution)/shard_map/dot_general | solution.py:37
  649.6 149.4 %all-gather.23.cloned.1.call-done = bf16[1536,8960]{0,1:T(8,128)(2,1)} async-done(((bf16[1536,280]{0,1:T(8,128)(2,1)}), bf16[1536,8960]{0,1:T(8,128)(2,1)}) %all-gather.23.cloned.1.call-update) | async-done | bytes 27525136 | tf_op jit(solution)/shard_map/all_gather | solution.py:186
  799.0 20.0 %multiply_convert_fusion = (bf16[256,8960]{1,0:T(8,128)(2,1)S(1)}, bf16[256,8960]{1,0:T(8,128)(2,1)}, bf16[256,8960]{1,0:T(8,128)(2,1)}) fusion(f32[256,8960]{1,0:T(8,128)} %fusion.52, f32[256,8960]{1,0:T(8,128)} %fusion.53, bf16[256,1536]{1,0:T(8,128)(2,1)S(1)} %copy-done.25, bf16[1536,8960]{0,1:T(8,128)(2,1)} %all-gather.23.cloned.1.call-done), kind=kOutput, calls=%fused_computation.1 | convolution fusion | flops 7083130880 | bytes 60424192 | tf_op jit(solution)/shard_map/dot_general | solution.py:43
  819.1 16.4 fusion.54
  835.5 14.8 multiply_reduce_fusion
  909.2 24.1 %all-to-all-done = bf16[256,4,384]{0,1,2:T(4,128)(2,1)S(1)} async-done(((bf16[256,4,384]{0,1,2:T(4,128)(2,1)}), bf16[256,4,384]{0,1,2:T(4,128)(2,1)S(1)}, u32[]{:S(2)}, u32[]{:S(2)}) %all-to-all-start) | async-done | bytes 786464 | tf_op jit(solution)/shard_map/all_to_all | solution.py:318
  941.5 23.7 %all-to-all-done.3 = bf16[256,4,384]{0,1,2:T(4,128)(2,1)S(1)} async-done(((bf16[256,4,384]{0,1,2:T(4,128)(2,1)}), bf16[256,4,384]{0,1,2:T(4,128)(2,1)S(1)}, u32[]{:S(2)}, u32[]{:S(2)}) %all-to-all-start.3) | async-done | bytes 786464 | tf_op jit(solution)/shard_map/all_to_all | solution.py:315
  986.1 18.3 %copy.199 = bf16[256,4,2240]{0,1,2:T(4,128)(2,1)} copy(bf16[256,4,2240]{0,2,1:T(8,128)(2,1)} %bitcast.331) | data formatting | bytes 9175040 | tf_op jit(solution)/shard_map/reshape | solution.py:48
  1011.3 146.0 %collective-permute-done = bf16[256,1536]{1,0:T(8,128)(2,1)S(1)} collective-permute-done((bf16[256,1536]{1,0:T(8,128)(2,1)S(1)}, bf16[256,1536]{1,0:T(8,128)(2,1)S(1)}, u32[]{:S(2)}, u32[]{:S(2)}) %collective-permute-start) | collective-permute-done | bytes 786464 | tf_op jit(solution)/shard_map/ppermute | solution.py:27
  1161.7 19.7 %collective-permute-done.1 = bf16[256,1536]{1,0:T(8,128)(2,1)S(1)} collective-permute-done((bf16[256,1536]{1,0:T(8,128)(2,1)S(1)}, bf16[256,1536]{1,0:T(8,128)(2,1)S(1)}, u32[]{:S(2)}, u32[]{:S(2)}) %collective-permute-start.1) | collective-permute-done | bytes 786464 | tf_op jit(solution)/shard_map/ppermute | solution.py:27
  1185.8 9.9 collective-permute-done.2
  1195.7 27.3 %collective-permute-start.3 = (bf16[256,1536]{1,0:T(8,128)(2,1)}, bf16[256,1536]{1,0:T(8,128)(2,1)}, u32[]{:S(2)}, u32[]{:S(2)}) collective-permute-start(bf16[256,1536]{1,0:T(8,128)(2,1)} %collective-permute-done.2), channel_id=1, source_target_pairs={{0,1},{1,2},{2,3},{3,4},{4,5},{5,6},{6,7},{7,0},{8,9},{9,10},{10,1... | collective-permute-start | bytes 2359304 | tf_op jit(solution)/shard_map/ppermute | solution.py:27
  1242.8 18.3 %copy.203 = bf16[256,4,2240]{0,1,2:T(4,128)(2,1)} copy(bf16[256,4,2240]{0,2,1:T(8,128)(2,1)} %bitcast.332) | data formatting | bytes 9175040 | tf_op jit(solution)/shard_map/reshape | solution.py:48
  1266.3 73.4 %all-to-all-start.5 = ((bf16[256,4,2240]{0,1,2:T(4,128)(2,1)}), bf16[256,4,2240]{0,1,2:T(4,128)(2,1)}, u32[]{:S(2)}, u32[]{:S(2)}) async-start(bf16[256,4,2240]{0,1,2:T(4,128)(2,1)} %copy.203), calls=%async_computation.9 | async-start | bytes 9175040 | tf_op jit(solution)/shard_map/all_to_all | solution.py:231
  1372.0 12.1 convolution_convert_fusion.2
  1390.6 18.2 %copy.207 = bf16[256,4,2240]{0,1,2:T(4,128)(2,1)} copy(bf16[256,4,2240]{0,2,1:T(8,128)(2,1)} %bitcast.336) | data formatting | bytes 9175040 | tf_op jit(solution)/shard_map/reshape | solution.py:48
  1408.8 33.4 %all-to-all-done.5 = bf16[256,4,2240]{0,1,2:T(4,128)(2,1)} async-done(((bf16[256,4,2240]{0,1,2:T(4,128)(2,1)}), bf16[256,4,2240]{0,1,2:T(4,128)(2,1)}, u32[]{:S(2)}, u32[]{:S(2)}) %all-to-all-start.5) | async-done | bytes 4587552 | tf_op jit(solution)/shard_map/all_to_all | solution.py:231
  1452.0 8.8 convolution_convert_fusion.1
  1461.0 88.4 %all-to-all-done.6 = bf16[256,4,2240]{0,1,2:T(4,128)(2,1)} async-done(((bf16[256,4,2240]{0,1,2:T(4,128)(2,1)}), bf16[256,4,2240]{0,1,2:T(4,128)(2,1)}, u32[]{:S(2)}, u32[]{:S(2)}) %all-to-all-start.6) | async-done | bytes 4587552 | tf_op jit(solution)/shard_map/all_to_all | solution.py:225
  1555.0 12.0 convolution_convert_fusion
  1574.9 15.0 fusion.19
  1598.9 38.4 %all-reduce.15 = (f32[1536]{0:T(1024)S(1)}, f32[1536]{0:T(1024)S(1)}) all-reduce(f32[1536]{0:T(1024)S(1)} %get-tuple-element.16, f32[1536]{0:T(1024)S(1)} %copy-done.56), channel_id=4, replica_groups=mesh['dp'=4,'seq'=8] {'dp','seq'}, use_global_device_ids=true, to_apply=%region_13.14.clone | all-reduce | flops 3072 | bytes 24576
  1642.7 9.7 all-reduce.17
  (379 shorter events, 262.4 us)
Async XLA Ops:
  7.2 144.3 %all-gather.11.cloned.1.call-start = ((), (), s32[]{:S(2)}) async-start(), calls=%async_computation.14 | async-start | bytes 1179648 | tf_op jit(solution)/shard_map/all_gather | solution.py:159
  101.6 67.4 %all-gather.13.cloned.1.call-start = ((), (), s32[]{:S(2)}) async-start(), calls=%async_computation.15 | async-start | bytes 1179648 | tf_op jit(solution)/shard_map/all_gather | solution.py:158
  146.8 87.7 %all-gather.15.cloned.1.call-start = ((), (), s32[]{:S(2)}) async-start(), calls=%async_computation.16 | async-start | bytes 4866048 | tf_op jit(solution)/shard_map/all_gather | solution.py:132
  147.5 151.7 %all-gather.17.cloned.1.call-start = ((), (), s32[]{:S(2)}) async-start(), calls=%async_computation.17 | async-start | bytes 4866048 | tf_op jit(solution)/shard_map/all_gather | solution.py:138
  148.1 317.8 %all-gather.19.cloned.1.call-start = ((), (), s32[]{:S(2)}) async-start(), calls=%async_computation.18 | async-start | bytes 28385280 | tf_op jit(solution)/shard_map/all_gather | solution.py:184
  148.7 483.7 %all-gather.21.cloned.1.call-start = ((), (), s32[]{:S(2)}) async-start(), calls=%async_computation.19 | async-start | bytes 28385280 | tf_op jit(solution)/shard_map/all_gather | solution.py:185
  149.3 649.7 %all-gather.23.cloned.1.call-start = ((), (), s32[]{:S(2)}) async-start(), calls=%async_computation.20 | async-start | bytes 28385280 | tf_op jit(solution)/shard_map/all_gather | solution.py:186
  150.0 787.2 %reduce-scatter.14.cloned.1.call-start = ((), (), s32[]{:S(2)}) async-start(), calls=%async_computation.21 | async-start | bytes 2359296 | tf_op jit(solution)/shard_map/reduce_scatter | solution.py:292
  877.4 91.2 %reduce-scatter.16.cloned.1.call-start = ((), (), s32[]{:S(2)}) async-start(), calls=%async_computation.22 | async-start | bytes 2359296 | tf_op jit(solution)/shard_map/reduce_scatter | solution.py:293
  893.5 367.8 %all-gather.25.cloned.1.call-start = ((), (), s32[]{:S(2)}) async-start(), calls=%async_computation.23 | async-start | bytes 7077888 | tf_op jit(solution)/shard_map/all_gather | solution.py:213
  894.1 477.9 %all-gather.27.cloned.1.call-start = ((), (), s32[]{:S(2)}) async-start(), calls=%async_computation.26 | async-start | bytes 7077888 | tf_op jit(solution)/shard_map/all_gather | solution.py:215
  903.5 29.8 %all-to-all-start = ((bf16[256,4,384]{0,1,2:T(4,128)(2,1)}), bf16[256,4,384]{0,1,2:T(4,128)(2,1)S(1)}, u32[]{:S(2)}, u32[]{:S(2)}) async-start(bf16[256,4,384]{0,1,2:T(4,128)(2,1)} %copy.184), calls=%async_computation.2 | async-start | bytes 1572864 | tf_op jit(solution)/shard_map/all_to_all | solution.py:318
  907.1 647.9 %all-gather.29.cloned.1.call-start = ((), (), s32[]{:S(2)}) async-start(), calls=%async_computation.27 | async-start | bytes 7077888 | tf_op jit(solution)/shard_map/all_gather | solution.py:216
  933.3 31.9 %all-to-all-start.3 = ((bf16[256,4,384]{0,1,2:T(4,128)(2,1)}), bf16[256,4,384]{0,1,2:T(4,128)(2,1)S(1)}, u32[]{:S(2)}, u32[]{:S(2)}) async-start(bf16[256,4,384]{0,1,2:T(4,128)(2,1)} %copy.193), calls=%async_computation.6 | async-start | bytes 1572864 | tf_op jit(solution)/shard_map/all_to_all | solution.py:315
  965.2 10.1 all-to-all-start.1
  975.3 29.1 %all-to-all-start.2 = ((bf16[256,4,64]{0,1,2:T(4,128)(2,1)}), bf16[256,4,64]{0,1,2:T(4,128)(2,1)}, u32[]{:S(2)}, u32[]{:S(2)}) async-start(bf16[256,4,64]{0,1,2:T(4,128)(2,1)} %copy.191), calls=%async_computation.5 | async-start | bytes 262144 | tf_op jit(solution)/shard_map/all_to_all | solution.py:324
  1004.4 261.9 %all-to-all-start.4 = ((bf16[256,4,2240]{0,1,2:T(4,128)(2,1)}), bf16[256,4,2240]{0,1,2:T(4,128)(2,1)}, u32[]{:S(2)}, u32[]{:S(2)}) async-start(bf16[256,4,2240]{0,1,2:T(4,128)(2,1)} %copy.199), calls=%async_computation.8 | async-start | bytes 9175040 | tf_op jit(solution)/shard_map/all_to_all | solution.py:228
  1009.6 581.1 %reduce-scatter.18.cloned.1.call-start = ((), (), s32[]{:S(2)}) async-start(), calls=%async_computation.24 | async-start | bytes 737280 | tf_op jit(solution)/shard_map/reduce_scatter | solution.py:336
  1010.9 146.4 %collective-permute-start = (bf16[256,1536]{1,0:T(8,128)(2,1)S(1)}, bf16[256,1536]{1,0:T(8,128)(2,1)S(1)}, u32[]{:S(2)}, u32[]{:S(2)}) collective-permute-start(bf16[256,1536]{1,0:T(8,128)(2,1)S(1)} %pad_maximum_fusion.3), channel_id=1, source_target_pairs={{0,1},{1,2},{2,3},{3,4},{4,5},{5,6},{6,7},{7,0},{8,9},{9,10},{10,1... | collective-permute-start | bytes 2359304 | tf_op jit(solution)/shard_map/ppermute | solution.py:27
  1158.2 23.2 %collective-permute-start.1 = (bf16[256,1536]{1,0:T(8,128)(2,1)S(1)}, bf16[256,1536]{1,0:T(8,128)(2,1)S(1)}, u32[]{:S(2)}, u32[]{:S(2)}) collective-permute-start(bf16[256,1536]{1,0:T(8,128)(2,1)S(1)} %collective-permute-done), channel_id=1, source_target_pairs={{0,1},{1,2},{2,3},{3,4},{4,5},{5,6},{6,7},{7,0},{8,9},{9,10},{10,1... | collective-permute-start | bytes 2359304 | tf_op jit(solution)/shard_map/ppermute | solution.py:27
  1158.2 24.1 %collective-permute-start.4 = (bf16[256,1536]{1,0:T(8,128)(2,1)S(1)}, bf16[256,1536]{1,0:T(8,128)(2,1)}, u32[]{:S(2)}, u32[]{:S(2)}) collective-permute-start(bf16[256,1536]{1,0:T(8,128)(2,1)S(1)} %pad_maximum_fusion.3), channel_id=1, source_target_pairs={{1,0},{2,1},{3,2},{4,3},{5,4},{6,5},{7,6},{0,7},{9,8},{10,9},{11,1... | collective-permute-start | bytes 2359304 | tf_op jit(solution)/shard_map/ppermute | solution.py:29
  1182.3 13.4 collective-permute-start.2
  1182.3 43.6 %collective-permute-start.5 = (bf16[256,1536]{1,0:T(8,128)(2,1)}, bf16[256,1536]{1,0:T(8,128)(2,1)}, u32[]{:S(2)}, u32[]{:S(2)}) collective-permute-start(bf16[256,1536]{1,0:T(8,128)(2,1)} %collective-permute-done.4), channel_id=1, source_target_pairs={{1,0},{2,1},{3,2},{4,3},{5,4},{6,5},{7,6},{0,7},{9,8},{10,9},{11,1... | collective-permute-start | bytes 2359304 | tf_op jit(solution)/shard_map/ppermute | solution.py:29
  1195.7 30.4 %collective-permute-start.3 = (bf16[256,1536]{1,0:T(8,128)(2,1)}, bf16[256,1536]{1,0:T(8,128)(2,1)}, u32[]{:S(2)}, u32[]{:S(2)}) collective-permute-start(bf16[256,1536]{1,0:T(8,128)(2,1)} %collective-permute-done.2), channel_id=1, source_target_pairs={{0,1},{1,2},{2,3},{3,4},{4,5},{5,6},{6,7},{7,0},{8,9},{9,10},{10,1... | collective-permute-start | bytes 2359304 | tf_op jit(solution)/shard_map/ppermute | solution.py:27
  1225.8 116.4 %collective-permute-start.6 = (bf16[256,1536]{1,0:T(8,128)(2,1)}, bf16[256,1536]{1,0:T(8,128)(2,1)}, u32[]{:S(2)}, u32[]{:S(2)}) collective-permute-start(bf16[256,1536]{1,0:T(8,128)(2,1)} %collective-permute-done.5), channel_id=1, source_target_pairs={{1,0},{2,1},{3,2},{4,3},{5,4},{6,5},{7,6},{0,7},{9,8},{10,9},{11,1... | collective-permute-start | bytes 2359304 | tf_op jit(solution)/shard_map/ppermute | solution.py:29
  1266.3 175.9 %all-to-all-start.5 = ((bf16[256,4,2240]{0,1,2:T(4,128)(2,1)}), bf16[256,4,2240]{0,1,2:T(4,128)(2,1)}, u32[]{:S(2)}, u32[]{:S(2)}) async-start(bf16[256,4,2240]{0,1,2:T(4,128)(2,1)} %copy.203), calls=%async_computation.9 | async-start | bytes 9175040 | tf_op jit(solution)/shard_map/all_to_all | solution.py:231
  1339.6 252.7 %reduce-scatter.20.cloned.1.call-start = ((), (), s32[]{:S(2)}) async-start(), calls=%async_computation.25 | async-start | bytes 737280 | tf_op jit(solution)/shard_map/reduce_scatter | solution.py:354
  1356.1 297.5 %all-reduce.21.cloned.1.call-start = ((), (), s32[]{:S(2)}) async-start(), calls=%async_computation.31 | async-start | bytes 393216
  1366.3 288.7 %reduce-scatter.22.cloned.1.call-start = ((), (), s32[]{:S(2)}) async-start(), calls=%async_computation.28 | async-start | bytes 4300800
  1442.2 107.2 %all-to-all-start.6 = ((bf16[256,4,2240]{0,1,2:T(4,128)(2,1)}), bf16[256,4,2240]{0,1,2:T(4,128)(2,1)}, u32[]{:S(2)}, u32[]{:S(2)}) async-start(bf16[256,4,2240]{0,1,2:T(4,128)(2,1)} %copy.207), calls=%async_computation.10 | async-start | bytes 9175040 | tf_op jit(solution)/shard_map/all_to_all | solution.py:225
  1446.9 210.6 %reduce-scatter.24.cloned.1.call-start = ((), (), s32[]{:S(2)}) async-start(), calls=%async_computation.29 | async-start | bytes 4300800
  1460.8 199.4 %reduce-scatter.26.cloned.1.call-start = ((), (), s32[]{:S(2)}) async-start(), calls=%async_computation.30 | async-start | bytes 4300800
  (72 other events, 3305.7 us)
Sparse Core Ops, SparseCore 0:
  101.7 21.1 all-gather.10
  146.9 22.0 all-gather.12
  172.1 62.3 all-gather.14
  237.3 61.9 all-gather.16
  302.2 163.6 all-gather.18
  468.8 163.5 all-gather.20
  635.4 163.5 all-gather.22
  877.5 34.3 reduce-scatter.13
  914.2 40.8 reduce-scatter.15
  956.6 97.0 all-gather.24
  1055.9 159.6 all-gather.26
  1217.1 74.5 all-gather.28
  1295.1 66.5 reduce-scatter.17
  1364.4 25.4 reduce-scatter.19
  1392.6 42.6 all-reduce.20
  1438.3 46.3 reduce-scatter.21
  1487.5 46.3 reduce-scatter.23
  1567.1 45.9 reduce-scatter.25
